TPU v7x, 32 devices: a whole 2x2x4 slice. The times are simulated.
32 devices in a mesh: row: 4 (over z), col: 8 (over y, x, core).
Axes of the slice: x: 2, y: 2, z: 4, core: 2. Of those that a mesh axis runs over, the one named last changes fastest.
Arguments:
- examples: bfloat16 [65536, 1024], P(('row', 'col')), may hold values from -20 to 20
- residuals: float32 [65536, 256], P(('row', 'col')), may hold values from -6 to 6
- coefficients: float32 [65536, 256], P(('row', 'col')), may hold values from -0.8 to 0.8
- block_index: int32 [1], replicated, may hold values from 0 to 63
Outputs:
- new_residuals: float32 [65536, 256], P(('row', 'col'))
- new_coefficients: float32 [65536, 256], P(('row', 'col'))
All inputs are finite; a program needn't handle non-finite values.
Results may differ from a plain program's by a relative error of at most 0.00035.
Values may be sent and summed in bfloat16 or wider, within the bound.
No kernel may reach another device: no remote copies, remote signals or barrier semaphores. Data moves between devices by JAX's collectives and lax.ppermute only.
A program may use at most 128 MiB of HBM per device.

v0:
```python
import jax
import jax.numpy as jnp
from jax import lax
from jax.sharding import PartitionSpec as P

BLOCK = 1024
ridge = 0.001
width_factor = 0.5


def spread(value, axis, source):
    kept = jnp.where(lax.axis_index(axis) == source, value, 0).astype(value.dtype)
    return lax.psum(kept, axis)


def body(examples, residuals, coefficients, block_index):
    rows_here = examples.shape[0]
    features = examples.shape[1]
    per_device = rows_here // BLOCK
    devices_all = lax.axis_size(("row", "col"))
    total_examples = rows_here * devices_all
    chosen = block_index[0]
    owner_rank = chosen // per_device
    offset = chosen % per_device * BLOCK
    my_rank = lax.axis_index(("row", "col"))
    is_owner = owner_rank == my_rank
    my_block = lax.dynamic_slice_in_dim(examples, offset, BLOCK, 0)
    block_rows = spread(my_block, ("row", "col"), owner_rank)
    sq_rows = jnp.sum(jnp.square(examples.astype(jnp.float32)), axis=1)
    sq_block = jnp.sum(jnp.square(block_rows.astype(jnp.float32)), axis=1)
    inner = lax.dot_general(
        examples, block_rows, (((1,), (1,)), ((), ())), preferred_element_type=jnp.float32
    )
    kernel = jnp.exp(
        -width_factor * (sq_rows[:, None] + sq_block[None, :] - 2.0 * inner) / features
    ).astype(jnp.bfloat16)
    residual_low = residuals.astype(jnp.bfloat16)
    grad_part = lax.dot_general(
        kernel, residual_low, (((0,), (0,)), ((), ())), preferred_element_type=jnp.float32
    )
    gram_part = lax.dot_general(
        kernel, kernel, (((0,), (0,)), ((), ())), preferred_element_type=jnp.float32
    )
    own_coef = lax.dynamic_slice_in_dim(coefficients, offset, BLOCK, 0)
    weight_own = jnp.where(is_owner, total_examples * ridge, 0.0).astype(jnp.float32)
    grad_part = grad_part - weight_own * own_coef
    grad, gram_sum = lax.psum((grad_part, gram_part), ("row", "col"))
    system = gram_sum / total_examples + ridge * jnp.eye(BLOCK, dtype=jnp.float32)
    factor = jnp.linalg.cholesky(system)
    update = jax.scipy.linalg.cho_solve((factor, True), grad / total_examples)
    update_low = update.astype(jnp.bfloat16)
    new_residuals = residuals - jnp.dot(kernel, update_low, preferred_element_type=jnp.float32)
    updated = lax.dynamic_update_slice_in_dim(coefficients, own_coef + update, offset, 0)
    new_coefficients = jnp.where(is_owner, updated, coefficients)
    return (new_residuals, new_coefficients)


def solution(mesh):
    in_specs = (P(("row", "col"), None), P(("row", "col"), None), P(("row", "col"), None), P())
    out_specs = (P(("row", "col"), None), P(("row", "col"), None))
    return jax.shard_map(body, mesh=mesh, in_specs=in_specs, out_specs=out_specs, check_vma=False)
```

profile of v0, /device:TPU:0, one launch (start us, length us, event | category | flops | bytes accessed | tf_op | source)
XLA Modules:
  0.0 689.6 jit_solution(11509813493711825370)
XLA Ops:
  7.2 1.6 copy.99
  9.5 3.4 dynamic-slice_select_fusion
  13.0 3.1 multiply_reduce_fusion
  16.1 135.1 %all-reduce.5.cloned.1.call-done = bf16[1024,1024]{1,0:T(8,128)(2,1)} async-done(((bf16[1024,1024]{1,0:T(8,128)(2,1)}), bf16[1024,1024]{1,0:T(8,128)(2,1)}) %all-reduce.5.cloned.1.call-update) | async-done | bytes 2097168 | tf_op jit(solution)/shard_map/psum | solution.py:13
  151.2 2.1 multiply_reduce_fusion.1
  153.3 7.9 %fusion.2 = bf16[2048,1024]{0,1:T(8,128)(2,1)S(1)} fusion(bf16[1024,1024]{1,0:T(8,128)(2,1)} %all-reduce.5.cloned.1.call-done, bf16[2048,1024]{1,0:T(8,128)(2,1)} %param.4, f32[1024]{0:T(1024)S(1)} %multiply_reduce_fusion.1, f32[2048]{0:T(1024)S(1)} %multiply_reduce_fusion), kind=kOutput, calls=%fused_computation.5 | convolution fusion | flops 4305453056 | bytes 10498048 | tf_op jit(solution)/shard_map/dot_general | solution.py:31
  161.2 6.1 fusion.101
  167.2 2.2 convolution_subtract_fusion.1
  169.5 147.1 %all-reduce.7.cloned.1.call-done = (f32[1024,256]{1,0:T(8,128)}, f32[1024,1024]{0,1:T(8,128)}) async-done(((f32[1024,256]{1,0:T(8,128)}, f32[1024,1024]{0,1:T(8,128)}), (f32[1024,256]{1,0:T(8,128)}, f32[1024,1024]{0,1:T(8,128)})) %all-reduce.7.cloned.1.call-update) | async-done | bytes 5242896 | tf_op jit(solution)/shard_map/psum | solution.py:47
  316.6 5.0 select_add_fusion
  321.6 5.5 copy.7
  327.1 4.5 fusion.3
  331.5 2.0 copy-done.1
  333.5 11.7 %cholesky.222 = f32[128,128]{1,0:T(8,128)S(1)} custom-call(f32[128,128]{1,0:T(8,128)S(1)} %cholesky.577), custom_call_target="Cholesky" | custom-call | tf_op jit(solution)/shard_map/jit(cholesky)/cholesky | solution.py:49
  345.4 9.8 %custom-call.66 = f32[1,128,128]{1,2,0:T(8,128)S(1)} custom-call(f32[1,128,128]{2,1,0:T(8,128)S(1)} %get-tuple-element.56), custom_call_target="InvertDiagBlocksLowerTriangular" | custom-call | tf_op jit(solution)/shard_map/jit(cholesky)/cholesky | solution.py:49
  355.2 1.5 fusion.29
  356.9 1.6 convolution_subtract_fusion.2
  359.3 11.7 %cholesky.243 = f32[128,128]{1,0:T(8,128)S(1)} custom-call(f32[128,128]{1,0:T(8,128)S(1)} %cholesky.581), custom_call_target="Cholesky" | custom-call | tf_op jit(solution)/shard_map/jit(cholesky)/cholesky | solution.py:49
  371.3 2.5 cholesky.254
  373.8 9.8 %custom-call.67 = f32[1,128,128]{1,2,0:T(8,128)S(1)} custom-call(f32[1,128,128]{2,1,0:T(8,128)S(1)} %get-tuple-element.54), custom_call_target="InvertDiagBlocksLowerTriangular" | custom-call | tf_op jit(solution)/shard_map/jit(cholesky)/cholesky | solution.py:49
  385.2 1.3 convolution_dynamic-update-slice_fusion
  386.5 2.7 convolution_subtract_fusion.3
  389.2 11.7 %cholesky.466 = f32[128,128]{1,0:T(8,128)S(1)} custom-call(f32[128,128]{1,0:T(8,128)S(1)} %cholesky.586), custom_call_target="Cholesky" | custom-call | tf_op jit(solution)/shard_map/jit(cholesky)/cholesky | solution.py:49
  401.7 9.8 %custom-call.68 = f32[1,128,128]{1,2,0:T(8,128)S(1)} custom-call(f32[1,128,128]{2,1,0:T(8,128)S(1)} %get-tuple-element.52), custom_call_target="InvertDiagBlocksLowerTriangular" | custom-call | tf_op jit(solution)/shard_map/jit(cholesky)/cholesky | solution.py:49
  411.5 1.2 convolution_dynamic-update-slice_fusion.1
  412.7 3.5 convolution_subtract_fusion.4
  416.3 11.7 %cholesky.485 = f32[128,128]{1,0:T(8,128)S(1)} custom-call(f32[128,128]{1,0:T(8,128)S(1)} %cholesky.591), custom_call_target="Cholesky" | custom-call | tf_op jit(solution)/shard_map/jit(cholesky)/cholesky | solution.py:49
  428.7 9.8 %custom-call.69 = f32[1,128,128]{1,2,0:T(8,128)S(1)} custom-call(f32[1,128,128]{2,1,0:T(8,128)S(1)} %get-tuple-element.50), custom_call_target="InvertDiagBlocksLowerTriangular" | custom-call | tf_op jit(solution)/shard_map/jit(cholesky)/cholesky | solution.py:49
  438.6 1.1 convolution_dynamic-update-slice_fusion.2
  439.7 3.2 convolution_subtract_fusion.5
  442.9 11.9 %cholesky.504 = f32[128,128]{1,0:T(8,128)S(1)} custom-call(f32[128,128]{1,0:T(8,128)S(1)} %cholesky.596), custom_call_target="Cholesky" | custom-call | tf_op jit(solution)/shard_map/jit(cholesky)/cholesky | solution.py:49
  455.5 9.8 %custom-call.70 = f32[1,128,128]{1,2,0:T(8,128)S(1)} custom-call(f32[1,128,128]{2,1,0:T(8,128)S(1)} %get-tuple-element.48), custom_call_target="InvertDiagBlocksLowerTriangular" | custom-call | tf_op jit(solution)/shard_map/jit(cholesky)/cholesky | solution.py:49
  465.3 1.1 convolution_dynamic-update-slice_fusion.3
  466.5 3.2 convolution_subtract_fusion.6
  469.7 11.7 %cholesky.524 = f32[128,128]{1,0:T(8,128)S(1)} custom-call(f32[128,128]{1,0:T(8,128)S(1)} %cholesky.601), custom_call_target="Cholesky" | custom-call | tf_op jit(solution)/shard_map/jit(cholesky)/cholesky | solution.py:49
  482.2 9.8 %custom-call.71 = f32[1,128,128]{1,2,0:T(8,128)S(1)} custom-call(f32[1,128,128]{2,1,0:T(8,128)S(1)} %get-tuple-element.46), custom_call_target="InvertDiagBlocksLowerTriangular" | custom-call | tf_op jit(solution)/shard_map/jit(cholesky)/cholesky | solution.py:49
  492.0 1.0 convolution_dynamic-update-slice_fusion.5
  493.0 3.1 convolution_subtract_fusion.19
  496.2 11.7 %cholesky.544 = f32[128,128]{1,0:T(8,128)S(1)} custom-call(f32[128,128]{1,0:T(8,128)S(1)} %cholesky.606), custom_call_target="Cholesky" | custom-call | tf_op jit(solution)/shard_map/jit(cholesky)/cholesky | solution.py:49
  508.6 9.8 %custom-call.72 = f32[1,128,128]{1,2,0:T(8,128)S(1)} custom-call(f32[1,128,128]{2,1,0:T(8,128)S(1)} %get-tuple-element.44), custom_call_target="InvertDiagBlocksLowerTriangular" | custom-call | tf_op jit(solution)/shard_map/jit(cholesky)/cholesky | solution.py:49
  519.4 2.2 convolution_subtract_fusion.22
  521.6 11.7 %cholesky.562 = f32[128,128]{1,0:T(8,128)S(1)} custom-call(f32[128,128]{1,0:T(8,128)S(1)} %convolution_subtract_fusion.22), custom_call_target="Cholesky" | custom-call | tf_op jit(solution)/shard_map/jit(cholesky)/cholesky | solution.py:49
  533.4 1.3 broadcast_multiply_fusion
  545.0 4.9 select_select_fusion
  549.9 28.3 %while.1 = (s32[]{:T(128)}, f32[1024,1024]{0,1:T(8,128)}, s32[8,2]{0,1:T(2,128)S(1)}, f32[8,128,128]{2,1,0:T(8,128)}, s32[]{:T(128)}) while((s32[]{:T(128)}, f32[1024,1024]{0,1:T(8,128)}, s32[8,2]{0,1:T(2,128)S(1)}, f32[8,128,128]{2,1,0:T(8,128)}, s32[]{:T(128)}) %tuple.53), condition=%wide.while_cond, body=%wide.while_body.sunk | while | flops 2 | bytes 393329 | solution.py:50
  550.5 2.2 dynamic-slice.9
  554.0 2.2 dynamic-slice.9
  557.6 2.2 dynamic-slice.9
  561.1 2.2 dynamic-slice.9
  564.7 2.2 dynamic-slice.9
  568.2 2.2 dynamic-slice.9
  571.8 2.2 dynamic-slice.9
  575.3 2.1 dynamic-slice.9
  578.2 80.2 %custom-call.73 = f32[8,128,128]{1,2,0:T(8,128)} custom-call(f32[8,128,128]{2,1,0:T(8,128)} %get-tuple-element.9), custom_call_target="InvertDiagBlocksLowerTriangular" | custom-call | tf_op jit(solution)/shard_map/jit(_cho_solve)/triangular_solve | solution.py:50
  658.4 1.3 constant_dynamic-update-slice_fusion.10
  659.7 1.3 convolution_subtract_fusion.18
  661.0 1.2 constant_dynamic-update-slice_fusion.9
  662.2 1.3 convolution_subtract_fusion.14
  663.5 1.2 constant_dynamic-update-slice_fusion.8
  664.6 1.4 convolution_subtract_fusion.13
  666.1 1.2 constant_dynamic-update-slice_fusion.7
  670.5 1.0 convolution_subtract_fusion.21
  678.2 2.8 convolution_subtract_fusion
  681.2 1.3 copy-done.4
  (142 shorter events, 33.8 us)
Async XLA Ops:
  7.2 144.0 %all-reduce.5.cloned.1.call-start = ((), (), s32[]{:S(2)}) async-start(), calls=%async_computation | async-start | bytes 4194304 | tf_op jit(solution)/shard_map/psum | solution.py:13
  13.0 303.6 %all-reduce.7.cloned.1.call-start = ((), (), s32[]{:S(2)}) async-start(), calls=%async_computation.1 | async-start | bytes 10485760 | tf_op jit(solution)/shard_map/psum | solution.py:47
  161.1 6.1 copy-start.2
  161.1 6.1 copy-start.5
  331.5 2.0 copy-start.1
  358.5 0.8 copy-start.8
  359.3 25.9 %copy-start.9 = (f32[896,128]{1,0:T(8,128)S(1)}, f32[896,128]{1,0:T(8,128)}, u32[]{:S(2)}) copy-start(f32[896,128]{1,0:T(8,128)} %copy-done.8) | copy-start | bytes 1376260
  658.4 8.8 %copy-start = (f32[1024,1024]{0,1:T(8,128)S(1)}, f32[1024,1024]{0,1:T(8,128)}, u32[]{:S(2)}) copy-start(f32[1024,1024]{0,1:T(8,128)} %get-tuple-element.124) | copy-start | bytes 12582916
  658.4 9.5 %copy-start.7 = (f32[8,128,128]{1,2,0:T(8,128)S(1)}, f32[8,128,128]{1,2,0:T(8,128)}, u32[]{:S(2)}) copy-start(f32[8,128,128]{1,2,0:T(8,128)} %custom-call.73) | copy-start | bytes 1572868
  675.4 2.2 copy-start.3
  675.4 2.9 copy-start.6
  681.2 1.3 copy-start.4
Sparse Core Ops, SparseCore 0:
  13.9 137.2 all-reduce.4
  169.6 146.9 all-reduce.6
where the time goes:
time: 698 us; the launch traced here: 690 us
  waiting for transfers between devices  282 us (40%)
  other arithmetic  272 us (39%)
  matrix products  65 us (9%)
  local copies, waits for them, and re-layouts  49.5 us (7%)
  between operations  20.7 us (3%)
    another operation x30, other arithmetic, body(): factor = jnp.linalg.cholesky(system)  167 us
    psum x1, waiting for transfers between devices, body(): grad, gram_sum = lax.psum((grad_part, gram_part), ('row', 'col'))  147 us
    psum x1, waiting for transfers between devices, spread(): return lax.psum(kept, axis)  135 us
    another operation x3, other arithmetic, body(): update = jax.scipy.linalg.cho_solve((factor, True), grad / total_examples)  85.1 us
    another operation x40, local copies, waits for them, and re-layouts  28.2 us
    another operation x14, matrix products, body(): factor = jnp.linalg.cholesky(system)  27.7 us
    another operation x30, matrix products, body(): update = jax.scipy.linalg.cho_solve((factor, True), grad / total_examples)  18.3 us
  transfers between devices with their start and end apart: 2, of which 2 were waited for; matrix products, arithmetic and copies ran while one was open for 0% of the time, Pallas kernels for 0%

commit v1 on v0

--- a/solution.py
+++ b/solution.py
@@ -6,6 +6,11 @@
 BLOCK = 1024
 ridge = 0.001
 width_factor = 0.5
+
+
+def axis_by_axis(value_2, first, second):
+    half = lax.psum(value_2, first)
+    return lax.psum(half, second)
 
 
 def spread(value, axis, source):
@@ -44,7 +49,7 @@
     own_coef = lax.dynamic_slice_in_dim(coefficients, offset, BLOCK, 0)
     weight_own = jnp.where(is_owner, total_examples * ridge, 0.0).astype(jnp.float32)
     grad_part = grad_part - weight_own * own_coef
-    grad, gram_sum = lax.psum((grad_part, gram_part), ("row", "col"))
+    grad, gram_sum = axis_by_axis((grad_part, gram_part), "col", "row")
     system = gram_sum / total_examples + ridge * jnp.eye(BLOCK, dtype=jnp.float32)
     factor = jnp.linalg.cholesky(system)
     update = jax.scipy.linalg.cho_solve((factor, True), grad / total_examples)

time: 698 us -> 834 us (1.19)
  waiting for transfers between devices: 282 us -> 418 us
    psum x1 -> x2, waiting for transfers between devices: 147 us -> 283 us  [the longest x1 191 us: axis_by_axis(): return lax.psum(half, second)]
  transfers between devices with their start and end apart: 2 -> 3, of which waited for: 2 -> 3; matrix products, arithmetic and copies ran while one was open for 0% -> 0% of each run, Pallas kernels for 0% -> 0%
where the time goes in v1:
time: 834 us; the launch traced here: 825 us
  waiting for transfers between devices  418 us (50%)
  other arithmetic  272 us (33%)
  matrix products  65 us (8%)
  local copies, waits for them, and re-layouts  49.5 us (6%)
  between operations  20.4 us (2%)
    psum x1, waiting for transfers between devices, axis_by_axis(): return lax.psum(half, second)  191 us
    another operation x30, other arithmetic, body(): factor = jnp.linalg.cholesky(system)  167 us
    psum x1, waiting for transfers between devices, spread(): return lax.psum(kept, axis)  135 us
    psum x1, waiting for transfers between devices, axis_by_axis(): half = lax.psum(value_2, first)  91.2 us
    another operation x3, other arithmetic, body(): update = jax.scipy.linalg.cho_solve((factor, True), grad / total_examples)  85.1 us
    another operation x40, local copies, waits for them, and re-layouts  28.2 us
    another operation x14, matrix products, body(): factor = jnp.linalg.cholesky(system)  27.7 us
    another operation x30, matrix products, body(): update = jax.scipy.linalg.cho_solve((factor, True), grad / total_examples)  18.3 us
  transfers between devices with their start and end apart: 3, of which 3 were waited for; matrix products, arithmetic and copies ran while one was open for 0% of the time, Pallas kernels for 0%

profile of v1, /device:TPU:0, one launch (start us, length us, event | category | flops | bytes accessed | tf_op | source)
XLA Modules:
  0.0 825.0 jit_solution(1578960839506162668)
XLA Ops:
  7.2 1.6 copy.101
  9.5 3.4 dynamic-slice_select_fusion
  13.0 3.1 multiply_reduce_fusion
  16.1 135.1 %all-reduce.7.cloned.1.call-done = bf16[1024,1024]{1,0:T(8,128)(2,1)} async-done(((bf16[1024,1024]{1,0:T(8,128)(2,1)}), bf16[1024,1024]{1,0:T(8,128)(2,1)}) %all-reduce.7.cloned.1.call-update) | async-done | bytes 2097168 | tf_op jit(solution)/shard_map/psum | solution.py:18
  151.2 2.1 multiply_reduce_fusion.1
  153.3 7.9 fusion.2
  161.2 6.1 fusion.101
  167.3 2.2 convolution_subtract_fusion.1
  169.6 91.2 %all-reduce.9.cloned.1.call-done = (f32[1024,256]{1,0:T(8,128)}, f32[1024,1024]{0,1:T(8,128)}) async-done(((f32[1024,256]{1,0:T(8,128)}, f32[1024,1024]{0,1:T(8,128)}), (f32[1024,256]{1,0:T(8,128)}, f32[1024,1024]{0,1:T(8,128)})) %all-reduce.9.cloned.1.call-update) | async-done | bytes 5242896 | tf_op jit(solution)/shard_map/psum | solution.py:12
  260.9 191.5 %all-reduce.11.cloned.1.call-done = (f32[1024,256]{1,0:T(8,128)}, f32[1024,1024]{0,1:T(8,128)}) async-done(((f32[1024,256]{1,0:T(8,128)}, f32[1024,1024]{0,1:T(8,128)}), (f32[1024,256]{1,0:T(8,128)}, f32[1024,1024]{0,1:T(8,128)})) %all-reduce.11.cloned.1.call-update) | async-done | bytes 5242896 | tf_op jit(solution)/shard_map/psum | solution.py:13
  452.4 5.0 select_add_fusion
  457.4 5.5 copy.7
  462.9 4.5 fusion.3
  467.3 2.0 copy-done.1
  469.3 11.7 %cholesky.222 = f32[128,128]{1,0:T(8,128)S(1)} custom-call(f32[128,128]{1,0:T(8,128)S(1)} %cholesky.577), custom_call_target="Cholesky" | custom-call | tf_op jit(solution)/shard_map/jit(cholesky)/cholesky | solution.py:54
  481.2 9.8 %custom-call.66 = f32[1,128,128]{1,2,0:T(8,128)S(1)} custom-call(f32[1,128,128]{2,1,0:T(8,128)S(1)} %get-tuple-element.58), custom_call_target="InvertDiagBlocksLowerTriangular" | custom-call | tf_op jit(solution)/shard_map/jit(cholesky)/cholesky | solution.py:54
  491.0 1.5 fusion.29
  492.7 1.6 convolution_subtract_fusion.2
  495.0 11.7 %cholesky.243 = f32[128,128]{1,0:T(8,128)S(1)} custom-call(f32[128,128]{1,0:T(8,128)S(1)} %cholesky.581), custom_call_target="Cholesky" | custom-call | tf_op jit(solution)/shard_map/jit(cholesky)/cholesky | solution.py:54
  507.1 2.5 cholesky.254
  509.6 9.8 %custom-call.67 = f32[1,128,128]{1,2,0:T(8,128)S(1)} custom-call(f32[1,128,128]{2,1,0:T(8,128)S(1)} %get-tuple-element.56), custom_call_target="InvertDiagBlocksLowerTriangular" | custom-call | tf_op jit(solution)/shard_map/jit(cholesky)/cholesky | solution.py:54
  520.9 1.3 convolution_dynamic-update-slice_fusion
  522.3 2.7 convolution_subtract_fusion.3
  525.0 11.7 %cholesky.466 = f32[128,128]{1,0:T(8,128)S(1)} custom-call(f32[128,128]{1,0:T(8,128)S(1)} %cholesky.586), custom_call_target="Cholesky" | custom-call | tf_op jit(solution)/shard_map/jit(cholesky)/cholesky | solution.py:54
  537.5 9.8 %custom-call.68 = f32[1,128,128]{1,2,0:T(8,128)S(1)} custom-call(f32[1,128,128]{2,1,0:T(8,128)S(1)} %get-tuple-element.54), custom_call_target="InvertDiagBlocksLowerTriangular" | custom-call | tf_op jit(solution)/shard_map/jit(cholesky)/cholesky | solution.py:54
  547.3 1.2 convolution_dynamic-update-slice_fusion.1
  548.5 3.5 convolution_subtract_fusion.4
  552.0 11.7 %cholesky.485 = f32[128,128]{1,0:T(8,128)S(1)} custom-call(f32[128,128]{1,0:T(8,128)S(1)} %cholesky.591), custom_call_target="Cholesky" | custom-call | tf_op jit(solution)/shard_map/jit(cholesky)/cholesky | solution.py:54
  564.5 9.8 %custom-call.69 = f32[1,128,128]{1,2,0:T(8,128)S(1)} custom-call(f32[1,128,128]{2,1,0:T(8,128)S(1)} %get-tuple-element.52), custom_call_target="InvertDiagBlocksLowerTriangular" | custom-call | tf_op jit(solution)/shard_map/jit(cholesky)/cholesky | solution.py:54
  574.3 1.1 convolution_dynamic-update-slice_fusion.2
  575.5 3.2 convolution_subtract_fusion.5
  578.6 11.9 %cholesky.504 = f32[128,128]{1,0:T(8,128)S(1)} custom-call(f32[128,128]{1,0:T(8,128)S(1)} %cholesky.596), custom_call_target="Cholesky" | custom-call | tf_op jit(solution)/shard_map/jit(cholesky)/cholesky | solution.py:54
  591.3 9.8 %custom-call.70 = f32[1,128,128]{1,2,0:T(8,128)S(1)} custom-call(f32[1,128,128]{2,1,0:T(8,128)S(1)} %get-tuple-element.50), custom_call_target="InvertDiagBlocksLowerTriangular" | custom-call | tf_op jit(solution)/shard_map/jit(cholesky)/cholesky | solution.py:54
  601.1 1.1 convolution_dynamic-update-slice_fusion.3
  602.2 3.2 convolution_subtract_fusion.6
  605.5 11.7 %cholesky.524 = f32[128,128]{1,0:T(8,128)S(1)} custom-call(f32[128,128]{1,0:T(8,128)S(1)} %cholesky.601), custom_call_target="Cholesky" | custom-call | tf_op jit(solution)/shard_map/jit(cholesky)/cholesky | solution.py:54
  618.0 9.8 %custom-call.71 = f32[1,128,128]{1,2,0:T(8,128)S(1)} custom-call(f32[1,128,128]{2,1,0:T(8,128)S(1)} %get-tuple-element.48), custom_call_target="InvertDiagBlocksLowerTriangular" | custom-call | tf_op jit(solution)/shard_map/jit(cholesky)/cholesky | solution.py:54
  627.8 1.0 convolution_dynamic-update-slice_fusion.5
  628.8 3.1 convolution_subtract_fusion.19
  631.9 11.7 %cholesky.544 = f32[128,128]{1,0:T(8,128)S(1)} custom-call(f32[128,128]{1,0:T(8,128)S(1)} %cholesky.606), custom_call_target="Cholesky" | custom-call | tf_op jit(solution)/shard_map/jit(cholesky)/cholesky | solution.py:54
  644.4 9.8 %custom-call.72 = f32[1,128,128]{1,2,0:T(8,128)S(1)} custom-call(f32[1,128,128]{2,1,0:T(8,128)S(1)} %get-tuple-element.46), custom_call_target="InvertDiagBlocksLowerTriangular" | custom-call | tf_op jit(solution)/shard_map/jit(cholesky)/cholesky | solution.py:54
  655.2 2.2 convolution_subtract_fusion.22
  657.4 11.7 %cholesky.562 = f32[128,128]{1,0:T(8,128)S(1)} custom-call(f32[128,128]{1,0:T(8,128)S(1)} %convolution_subtract_fusion.22), custom_call_target="Cholesky" | custom-call | tf_op jit(solution)/shard_map/jit(cholesky)/cholesky | solution.py:54
  669.2 1.3 broadcast_multiply_fusion
  680.8 4.9 select_select_fusion
  685.6 28.3 %while.1 = (s32[]{:T(128)}, f32[1024,1024]{0,1:T(8,128)}, s32[8,2]{0,1:T(2,128)S(1)}, f32[8,128,128]{2,1,0:T(8,128)}, s32[]{:T(128)}) while((s32[]{:T(128)}, f32[1024,1024]{0,1:T(8,128)}, s32[8,2]{0,1:T(2,128)S(1)}, f32[8,128,128]{2,1,0:T(8,128)}, s32[]{:T(128)}) %tuple.53), condition=%wide.while_cond, body=%wide.while_body.sunk | while | flops 2 | bytes 393329 | solution.py:55
  686.2 2.2 dynamic-slice.9
  689.8 2.2 dynamic-slice.9
  693.3 2.2 dynamic-slice.9
  696.9 2.2 dynamic-slice.9
  700.4 2.2 dynamic-slice.9
  704.0 2.2 dynamic-slice.9
  707.5 2.2 dynamic-slice.9
  711.1 2.1 dynamic-slice.9
  714.0 80.2 %custom-call.73 = f32[8,128,128]{1,2,0:T(8,128)} custom-call(f32[8,128,128]{2,1,0:T(8,128)} %get-tuple-element.9), custom_call_target="InvertDiagBlocksLowerTriangular" | custom-call | tf_op jit(solution)/shard_map/jit(_cho_solve)/triangular_solve | solution.py:55
  794.2 1.3 constant_dynamic-update-slice_fusion.10
  795.5 1.3 convolution_subtract_fusion.18
  796.8 1.2 constant_dynamic-update-slice_fusion.9
  797.9 1.3 convolution_subtract_fusion.14
  799.2 1.2 constant_dynamic-update-slice_fusion.8
  800.4 1.4 convolution_subtract_fusion.13
  801.8 1.2 constant_dynamic-update-slice_fusion.7
  814.0 2.8 convolution_subtract_fusion
  817.0 1.3 copy-done.4
  (145 shorter events, 34.8 us)
Async XLA Ops:
  7.2 144.0 %all-reduce.7.cloned.1.call-start = ((), (), s32[]{:S(2)}) async-start(), calls=%async_computation | async-start | bytes 4194304 | tf_op jit(solution)/shard_map/psum | solution.py:18
  13.0 247.9 %all-reduce.9.cloned.1.call-start = ((), (), s32[]{:S(2)}) async-start(), calls=%async_computation.1 | async-start | bytes 10485760 | tf_op jit(solution)/shard_map/psum | solution.py:12
  161.1 6.1 copy-start.2
  161.1 6.1 copy-start.5
  169.5 282.8 %all-reduce.11.cloned.1.call-start = ((), (), s32[]{:S(2)}) async-start(), calls=%async_computation.2 | async-start | bytes 10485760 | tf_op jit(solution)/shard_map/psum | solution.py:13
  467.3 2.0 copy-start.1
  494.3 0.8 copy-start.8
  495.0 25.9 %copy-start.9 = (f32[896,128]{1,0:T(8,128)S(1)}, f32[896,128]{1,0:T(8,128)}, u32[]{:S(2)}) copy-start(f32[896,128]{1,0:T(8,128)} %copy-done.8) | copy-start | bytes 1376260
  794.2 8.8 %copy-start = (f32[1024,1024]{0,1:T(8,128)S(1)}, f32[1024,1024]{0,1:T(8,128)}, u32[]{:S(2)}) copy-start(f32[1024,1024]{0,1:T(8,128)} %get-tuple-element.130) | copy-start | bytes 12582916
  794.2 9.5 %copy-start.7 = (f32[8,128,128]{1,2,0:T(8,128)S(1)}, f32[8,128,128]{1,2,0:T(8,128)}, u32[]{:S(2)}) copy-start(f32[8,128,128]{1,2,0:T(8,128)} %custom-call.73) | copy-start | bytes 1572868
  811.1 2.2 copy-start.3
  811.1 2.9 copy-start.6
  817.0 1.3 copy-start.4
Sparse Core Ops, SparseCore 0:
  13.9 137.2 all-reduce.6
  169.7 91.1 all-reduce.8
  263.3 189.0 all-reduce.10
